TPU v7x, 32 devices: a whole 2x2x4 slice. The times are simulated.
32 devices in a mesh: blk: 4 (over y, core), rows: 8 (over z, x).
Axes of the slice: x: 2, y: 2, z: 4, core: 2. Of those that a mesh axis runs over, the one named last changes fastest.
Arguments:
- section_weights: bfloat16 [4, 256, 9, 256], P('blk'), may hold values from -0.125 to 0.125
- grad_acc: bfloat16 [4, 256, 9, 256], P('blk', 'rows'), may hold values from -6 to 6
- saved_inputs: bfloat16 [3, 4, 32, 256, 256], P(None, 'blk', 'rows'), may hold values from -6 to 6
- cotangent: bfloat16 [4, 32, 256, 256], P('blk', 'rows'), may hold values from -6 to 6
- fresh_grads: bfloat16 [2, 32, 256, 256], P(None, 'rows'), may hold values from -6 to 6
Outputs:
- tick_states: bfloat16 [3, 4, 32, 256, 256], P(None, 'blk', 'rows')
- grad_out: bfloat16 [4, 256, 9, 256], P('blk', 'rows')
All inputs are finite; a program needn't handle non-finite values.
Results may differ from a plain program's by a relative error of at most 0.0057.
Values may be sent and summed in bfloat16 or wider, within the bound.
A program may use at most 128 MiB of HBM per device.

v0:
```python
import functools

import jax
import jax.numpy as jnp
from jax import lax
from jax.experimental import pallas as pl
from jax.experimental.pallas import tpu as pltpu
from jax.sharding import PartitionSpec as P

TICKS = 3
MESH = pl.DeviceIdType.MESH
F32 = jnp.float32
BF16 = jnp.bfloat16


def flipped(bits, value):
    return sum(((value >> k) & 1) << (bits - 1 - k) for k in range(bits))


def kernel(
    shape, w_hbm, acc_hbm, saved_hbm, cot_hbm, fresh_hbm, states_hbm, out_ref,
    kern, kern_t, sv, cur, fresh, xs, gs, halo, states, dk, rx, part, sib, held, held_rx,
    load_sem, halo_send, halo_recv, k_send, k_recv, rs_send, rs_recv, acc_send, acc_recv, sib_send, sib_recv, st_sem,
):
    peers, cycle, height, ch, cols, scale = shape
    bits = peers.bit_length() - 1
    row = lax.axis_index("rows")
    pos = lax.axis_index("blk")
    below = lax.rem(pos + cycle - 1, cycle)
    bit = [lax.rem(row // (1 << k), 2) for k in range(bits)]
    mate = [row + (1 - 2 * bit[k]) * (1 << k) for k in range(bits)]
    has_up = row > 0
    has_down = row < peers - 1
    restart = [None] + [pos == (cycle - t) % cycle for t in range(1, TICKS)]

    loads = [
        pltpu.make_async_copy(cot_hbm.at[0], cur.at[0], load_sem.at[0]),
        pltpu.make_async_copy(saved_hbm.at[0, 0], sv.at[0], load_sem.at[1]),
        pltpu.make_async_copy(w_hbm.at[0], kern.at[0], load_sem.at[2]),
        pltpu.make_async_copy(fresh_hbm, fresh, load_sem.at[3]),
        pltpu.make_async_copy(saved_hbm.at[1, 0], sv.at[1], load_sem.at[4]),
        pltpu.make_async_copy(saved_hbm.at[2, 0], sv.at[2], load_sem.at[5]),
        pltpu.make_async_copy(acc_hbm.at[0], held.at[0], load_sem.at[6]),
    ]
    for load in loads:
        load.start()

    barrier = pltpu.get_barrier_semaphore()
    core = lax.rem(pos, 2)
    sibling = pos + 1 - 2 * core
    far = lax.rem(pos + cycle - (TICKS - 1), cycle)
    hops = sorted({d % cycle for d in (1, -1, TICKS - 1, 1 - TICKS)})
    greet = [{"blk": lax.rem(pos + d, cycle)} for d in hops] + [{"rows": m} for m in mate]
    for who in greet:
        pl.semaphore_signal(barrier, inc=1, device_id=who, device_id_type=MESH)

    other = row + 2 * bit[0] - 1
    has_other = jnp.logical_and(other >= 0, other < peers)

    @pl.when(has_other)
    def _():
        pl.semaphore_signal(barrier, inc=1, device_id={"rows": other}, device_id_type=MESH)

    pl.semaphore_wait(barrier, len(greet) + has_other.astype(jnp.int32))

    def halo_copy(t, side):
        edge = 0 if side == 1 else height - 1
        return pltpu.make_async_remote_copy(
            src_ref=cur.at[t, edge],
            dst_ref=halo.at[t, side],
            send_sem=halo_send.at[t, side],
            recv_sem=halo_recv.at[t, side],
            device_id={"rows": row - 1 if side == 1 else row + 1},
            device_id_type=MESH,
        )

    def halo_start(t):
        @pl.when(has_up)
        def _():
            halo_copy(t, 1).start()

        @pl.when(has_down)
        def _():
            halo_copy(t, 0).start()

    def kern_copy(t):
        return pltpu.make_async_remote_copy(
            src_ref=kern.at[t],
            dst_ref=kern.at[t + 1],
            send_sem=k_send.at[t],
            recv_sem=k_recv.at[t],
            device_id={"blk": below},
            device_id_type=MESH,
        )

    held_copy = pltpu.make_async_remote_copy(
        src_ref=held.at[1],
        dst_ref=held_rx,
        send_sem=acc_send,
        recv_sem=acc_recv,
        device_id={"blk": far},
        device_id_type=MESH,
    )

    def sib_copy(a):
        return pltpu.make_async_remote_copy(
            src_ref=dk.at[1, a],
            dst_ref=sib.at[a],
            send_sem=sib_send.at[a],
            recv_sem=sib_recv.at[a],
            device_id={"blk": sibling},
            device_id_type=MESH,
        )

    wide = 3 * ch
    lane = lax.broadcasted_iota(jnp.int32, (ch, cols), 1)

    def put_row(index, value):
        base = pl.multiple_of(index * wide, wide)
        full = value.astype(F32)
        left = jnp.where(lane == cols - 1, 0.0, pltpu.roll(full, cols - 1, 1))
        right = jnp.where(lane == 0, 0.0, pltpu.roll(full, 1, 1))
        gs[pl.ds(base, ch), :] = left.astype(BF16)
        gs[pl.ds(base + ch, ch), :] = value
        gs[pl.ds(base + 2 * ch, ch), :] = right.astype(BF16)

    def inner_rows(t):
        def step(r, carry):
            put_row(r + 1, cur[t, r])
            return carry

        lax.fori_loop(0, height, step, 0)
        for r in range(height):
            xs[:, r * cols : (r + 1) * cols] = jnp.maximum(sv[t, r], 0)

    def outer_rows(t):
        for side, have, index in ((0, has_up, 0), (1, has_down, height + 1)):
            @pl.when(have)
            def _():
                halo_copy(t, side).wait_recv()
                put_row(index, halo[t, side])

            @pl.when(jnp.logical_not(have))
            def _():
                gs[index * wide : (index + 1) * wide, :] = jnp.zeros((wide, cols), BF16)

    def turn_kernel(t):
        for tap in range(9):
            a, b = tap // 3, tap % 3
            at = (2 - a) * wide + b * ch
            kern_t[:, at : at + ch] = kern[t, tap].T

    def back_row(t, r):
        base = pl.multiple_of(r * wide, wide)
        total = jnp.dot(kern_t[...], gs[pl.ds(base, 3 * wide), :], preferred_element_type=F32)
        value = jnp.where(sv[t, r].astype(F32) > 0, total, 0.0).astype(BF16)
        states[t, r] = value
        if t + 1 < TICKS:
            cur[t + 1, r] = jnp.where(restart[t + 1], fresh[t, r], value)

    def back(t):
        def outer(i, carry):
            back_row(t, i * (height - 1))
            return carry

        def inner(i, carry):
            back_row(t, i + 1)
            return carry

        lax.fori_loop(0, 2, outer, 0)
        if t + 1 < TICKS:
            halo_start(t + 1)
        lax.fori_loop(0, height - 2, inner, 0)
        pltpu.make_async_copy(states.at[t], states_hbm.at[t, 0], st_sem.at[t]).start()

    slab = ch // peers

    def weight_rows(t, a):
        left = jnp.concatenate(
            [gs[(r + 2 - a) * wide : (r + 3 - a) * wide, :] for r in range(height)], axis=1
        )
        total = lax.dot_general(left, xs[...], (((1,), (1,)), ((), ())), preferred_element_type=F32)
        total = total * scale
        for b in range(3):
            for j in range(peers):
                at = b * ch + j * slab
                value = total[at : at + slab, :]
                if t == TICKS - 1:
                    extra = sib[a, flipped(bits, j), b].astype(F32)
                    value = value + jnp.where(core == 0, extra, 0.0)
                dk[t, a, flipped(bits, j), b] = value.astype(BF16)

    def add_sibling(a):
        def step(j, carry):
            dk[0, a, j] = (dk[0, a, j].astype(F32) + sib[a, j].astype(F32)).astype(BF16)
            return carry

        lax.fori_loop(0, peers, step, 0)

    def rs_copy(t, a, k):
        count = peers >> (k + 1)
        source = dk.at[2 * t, a] if k == 0 else part.at[t, a, pl.ds(peers - (peers >> (k - 1)), peers >> k)]
        return pltpu.make_async_remote_copy(
            src_ref=source.at[pl.ds((1 - bit[k]) * count, count)],
            dst_ref=rx.at[t, a, pl.ds(peers - (peers >> k), count)],
            send_sem=rs_send.at[t, a, k],
            recv_sem=rs_recv.at[t, a, k],
            device_id={"rows": mate[k]},
            device_id_type=MESH,
        )

    def summed(t, a, k):
        count = peers >> (k + 1)
        rs_copy(t, a, k).wait_recv()
        at = bit[k] * count
        if k == 0:
            own = dk[2 * t, a, pl.ds(at, count)]
        else:
            own = part[t, a, pl.ds(at + peers - (peers >> (k - 1)), count)]
        return own.astype(F32) + rx[t, a, pl.ds(peers - (peers >> k), count)].astype(F32)

    def rs_step(t, a, k):
        count = peers >> (k + 1)
        part[t, a, pl.ds(peers - (peers >> k), count)] = summed(t, a, k).astype(BF16)
        rs_copy(t, a, k + 1).start()

    def rs_last(t, a):
        total = summed(t, a, bits - 1)[0]
        before = held[0, 3 * a : 3 * a + 3] if t == 0 else held_rx[3 * a : 3 * a + 3]
        value = (before.astype(F32) + total).astype(BF16)
        if t == 0:
            held[1, 3 * a : 3 * a + 3] = value
        else:
            out_ref[0, 3 * a : 3 * a + 3] = value

    order = (1, 0, 2)

    first = core == 0
    second = core == 1

    loads[0].wait()
    halo_start(0)
    loads[2].wait()
    kern_copy(0).start()
    turn_kernel(0)
    loads[1].wait()
    inner_rows(0)
    weight_rows(0, 1)

    @pl.when(first)
    def _():
        rs_copy(0, 1, 0).start()

    loads[3].wait()
    outer_rows(0)
    back(0)
    weight_rows(0, 0)
    weight_rows(0, 2)

    @pl.when(first)
    def _():
        rs_copy(0, 0, 0).start()
        rs_copy(0, 2, 0).start()

    loads[4].wait()
    inner_rows(1)
    weight_rows(1, 1)
    sib_copy(1).start()
    outer_rows(1)
    for a in (0, 2):
        weight_rows(1, a)
        sib_copy(a).start()
    for a in order:
        sib_copy(a).wait_recv()

        @pl.when(second)
        def _():
            add_sibling(a)
            rs_copy(0, a, 0).start()

    @pl.when(first)
    def _():
        for a in order:
            rs_step(0, a, 0)

    kern_copy(0).wait_recv()
    kern_copy(1).start()
    turn_kernel(1)
    back(1)
    loads[5].wait()
    loads[6].wait()
    inner_rows(2)
    weight_rows(2, 1)
    rs_copy(1, 1, 0).start()

    @pl.when(second)
    def _():
        for a in order:
            rs_step(0, a, 0)

    for k in range(1, bits - 1):
        for a in order:
            rs_step(0, a, k)
    outer_rows(2)
    for a in (0, 2):
        weight_rows(2, a)
        rs_copy(1, a, 0).start()
    for a in order:
        rs_last(0, a)
    held_copy.start()
    rs_step(1, 1, 0)
    kern_copy(1).wait_recv()
    turn_kernel(2)
    back(2)
    rs_step(1, 0, 0)
    for k in range(1, bits - 1):
        rs_step(1, 1, k)
    rs_step(1, 2, 0)
    for k in range(1, bits - 1):
        rs_step(1, 0, k)
        rs_step(1, 2, k)
    held_copy.wait_recv()
    for a in order:
        rs_last(1, a)

    for t in range(TICKS):
        pltpu.make_async_copy(states.at[t], states_hbm.at[t, 0], st_sem.at[t]).wait()
        @pl.when(has_up)
        def _():
            halo_copy(t, 1).wait_send()

        @pl.when(has_down)
        def _():
            halo_copy(t, 0).wait_send()

    for t in range(TICKS - 1):
        kern_copy(t).wait_send()
        for a in range(3):
            for k in range(bits):
                rs_copy(t, a, k).wait_send()
    for a in range(3):
        sib_copy(a).wait_send()
    held_copy.wait_send()


def shards(section_weights, grad_acc, saved_inputs, cotangent, fresh_grads):
    peers = lax.axis_size("rows")
    cycle = lax.axis_size("blk")
    ticks, _, height, ch, cols = saved_inputs.shape
    bits = peers.bit_length() - 1
    slab = ch // peers
    scale = float(peers * height * cols) ** (-0.5)
    weights = section_weights.transpose(0, 2, 1, 3)
    held = grad_acc.transpose(0, 2, 1, 3)
    anywhere = pl.BlockSpec(memory_space=pl.ANY)
    dma = pltpu.SemaphoreType.DMA
    states, out = pl.pallas_call(
        functools.partial(kernel, (peers, cycle, height, ch, cols, scale)),
        out_shape=(
            jax.ShapeDtypeStruct(saved_inputs.shape, BF16),
            jax.ShapeDtypeStruct(held.shape, BF16),
        ),
        in_specs=[anywhere] * 5,
        out_specs=(anywhere, pl.BlockSpec(memory_space=pltpu.VMEM)),
        scratch_shapes=[
            pltpu.VMEM((ticks, 9, ch, ch), BF16),
            pltpu.VMEM((ch, 9 * ch), BF16),
            pltpu.VMEM((ticks, height, ch, cols), BF16),
            pltpu.VMEM((ticks, height, ch, cols), BF16),
            pltpu.VMEM((ticks - 1, height, ch, cols), BF16),
            pltpu.VMEM((ch, height * cols), BF16),
            pltpu.VMEM(((height + 2) * 3 * ch, cols), BF16),
            pltpu.VMEM((ticks, 2, ch, cols), BF16),
            pltpu.VMEM((ticks, height, ch, cols), BF16),
            pltpu.VMEM((ticks, 3, peers, 3, slab, ch), BF16),
            pltpu.VMEM((2, 3, peers, 3, slab, ch), BF16),
            pltpu.VMEM((2, 3, peers, 3, slab, ch), BF16),
            pltpu.VMEM((3, peers, 3, slab, ch), BF16),
            pltpu.VMEM((2, 9, slab, ch), BF16),
            pltpu.VMEM((9, slab, ch), BF16),
            dma((7,)),
            dma((ticks, 2)),
            dma((ticks, 2)),
            dma((ticks - 1,)),
            dma((ticks - 1,)),
            dma((2, 3, bits)),
            dma((2, 3, bits)),
            dma,
            dma,
            dma((3,)),
            dma((3,)),
            dma((ticks,)),
        ],
        compiler_params=pltpu.CompilerParams(collective_id=0, has_side_effects=True),
    )(weights, held, saved_inputs, cotangent, fresh_grads)
    return states, out.transpose(0, 2, 1, 3)


def solution(mesh):
    return jax.shard_map(
        shards,
        mesh=mesh,
        in_specs=(
            P("blk", None, None, None),
            P("blk", "rows", None, None),
            P(None, "blk", "rows", None, None),
            P("blk", "rows", None, None),
            P(None, "rows", None, None),
        ),
        out_specs=(P(None, "blk", "rows", None, None), P("blk", "rows", None, None)),
        check_vma=False,
    )
```

profile of v0, /device:TPU:1, one launch (start us, length us, event | category | flops | bytes accessed | tf_op | source)
XLA Modules:
  0.0 60.3 jit_solution(18157411948693793558)
XLA Ops:
  0.6 56.3 %shard_map.68 = (bf16[3,1,4,256,256]{4,3,2,1,0:T(8,128)(2,1)}, bf16[1,9,32,256]{3,2,1,0:T(8,128)(2,1)}) custom-call(bf16[1,9,256,256]{3,2,1,0:T(8,128)(2,1)} %bitcast.3, bf16[1,9,32,256]{3,2,1,0:T(8,128)(2,1)} %bitcast.4, bf16[3,1,4,256,256]{4,3,2,1,0:T(8,128)(2,1)} %saved_hbm.1, bf16[1,4,256,256]{3,2,1,0:T(8,128)(2,1)} %cot_hbm.1, ...), custom_call_target="tpu_custom_call" | custom-call | tf_op jit(solution)/shard_map/pallas_call | solution.py:357
  56.9 0.0 copy-start
  56.9 2.7 %copy.9 = bf16[3,1,4,256,256]{4,3,2,1,0:T(8,128)(2,1)} copy(bf16[3,1,4,256,256]{4,3,2,1,0:T(8,128)(2,1)} %get-tuple-element.8) | data formatting | bytes 3145728
  59.6 0.0 copy-done
  59.6 0.7 %copy.10 = bf16[1,32,9,256]{3,1,2,0:T(8,128)(2,1)} copy(bf16[1,32,9,256]{3,1,2,0:T(8,128)(2,1)S(1)} %bitcast.5) | data formatting | bytes 294912
Async XLA Ops:
  56.9 2.7 %copy-start = (bf16[1,9,32,256]{3,2,1,0:T(8,128)(2,1)S(1)}, bf16[1,9,32,256]{3,2,1,0:T(8,128)(2,1)}, u32[]{:S(2)}) copy-start(bf16[1,9,32,256]{3,2,1,0:T(8,128)(2,1)} %get-tuple-element.5) | copy-start | bytes 442372
where the time goes:
time: 60.6 us; the launch traced here: 60.3 us
  Pallas kernels  56.3 us (93%)
  local copies, waits for them, and re-layouts  3.35 us (6%)
  between operations  0.65 us (1%)
    pallas_call x1, Pallas kernels, shards(): pl.pallas_call(functools.partial(kernel, (peers, cycle, height, ch, cols,...  56.3 us
    unnamed x4, local copies, waits for them, and re-layouts  3.35 us

commit v1 on v0

--- a/solution.py
+++ b/solution.py
@@ -13,8 +13,15 @@
 BF16 = jnp.bfloat16
 
 
-def flipped(bits, value):
-    return sum(((value >> k) & 1) << (bits - 1 - k) for k in range(bits))
+LATE = {(0, 0): (0, 1, 2), (0, 1): (0, 1, 2), (1, 0): (), (1, 1): ()}
+
+
+def halving(bits, t, core, a):
+    return [*range(1, bits), 0] if a in LATE[t, core] else list(range(bits))
+
+
+def place(bits, t, core, a, value):
+    return sum(((value >> k) & 1) << (bits - 1 - at) for at, k in enumerate(halving(bits, t, core, a)))
 
 
 def kernel(
@@ -158,22 +165,37 @@
         if t + 1 < TICKS:
             cur[t + 1, r] = jnp.where(restart[t + 1], fresh[t, r], value)
 
-    def back(t):
+    def back_edges(t):
         def outer(i, carry):
             back_row(t, i * (height - 1))
             return carry
 
+        lax.fori_loop(0, 2, outer, 0)
+        if t + 1 < TICKS:
+            halo_start(t + 1)
+
+    def back_rest(t):
         def inner(i, carry):
             back_row(t, i + 1)
             return carry
 
-        lax.fori_loop(0, 2, outer, 0)
-        if t + 1 < TICKS:
-            halo_start(t + 1)
         lax.fori_loop(0, height - 2, inner, 0)
         pltpu.make_async_copy(states.at[t], states_hbm.at[t, 0], st_sem.at[t]).start()
 
+    def back(t):
+        back_edges(t)
+        back_rest(t)
+
     slab = ch // peers
+
+    slot = (((0, 0), (0, 1)), ((0, 1), (1, 0)), ((1, 0), (1, 1)))
+
+    def pick(even, odd):
+        return even if even == odd else even + core * (odd - even)
+
+    def along(values, t, a, k):
+        even, odd = halving(bits, t, 0, a)[k], halving(bits, t, 1, a)[k]
+        return values[even] if even == odd else values[even] + core * (values[odd] - values[even])
 
     def weight_rows(t, a):
         left = jnp.concatenate(
@@ -185,10 +207,11 @@
             for j in range(peers):
                 at = b * ch + j * slab
                 value = total[at : at + slab, :]
+                at = pick(place(bits, *slot[t][0], a, j), place(bits, *slot[t][1], a, j))
                 if t == TICKS - 1:
-                    extra = sib[a, flipped(bits, j), b].astype(F32)
+                    extra = sib[a, at, b].astype(F32)
                     value = value + jnp.where(core == 0, extra, 0.0)
-                dk[t, a, flipped(bits, j), b] = value.astype(BF16)
+                dk[t, a, at, b] = value.astype(BF16)
 
     def add_sibling(a):
         def step(j, carry):
@@ -201,18 +224,18 @@
         count = peers >> (k + 1)
         source = dk.at[2 * t, a] if k == 0 else part.at[t, a, pl.ds(peers - (peers >> (k - 1)), peers >> k)]
         return pltpu.make_async_remote_copy(
-            src_ref=source.at[pl.ds((1 - bit[k]) * count, count)],
+            src_ref=source.at[pl.ds((1 - along(bit, t, a, k)) * count, count)],
             dst_ref=rx.at[t, a, pl.ds(peers - (peers >> k), count)],
             send_sem=rs_send.at[t, a, k],
             recv_sem=rs_recv.at[t, a, k],
-            device_id={"rows": mate[k]},
+            device_id={"rows": along(mate, t, a, k)},
             device_id_type=MESH,
         )
 
     def summed(t, a, k):
         count = peers >> (k + 1)
         rs_copy(t, a, k).wait_recv()
-        at = bit[k] * count
+        at = along(bit, t, a, k) * count
         if k == 0:
             own = dk[2 * t, a, pl.ds(at, count)]
         else:
@@ -246,31 +269,61 @@
     loads[1].wait()
     inner_rows(0)
     weight_rows(0, 1)
+    loads[3].wait()
 
     @pl.when(first)
     def _():
         rs_copy(0, 1, 0).start()
-
-    loads[3].wait()
+        kern_copy(0).wait_recv()
+        kern_copy(1).start()
+
     outer_rows(0)
-    back(0)
-    weight_rows(0, 0)
-    weight_rows(0, 2)
-
-    @pl.when(first)
-    def _():
-        rs_copy(0, 0, 0).start()
-        rs_copy(0, 2, 0).start()
-
+    back_edges(0)
+    for a in (0, 2):
+        weight_rows(0, a)
+
+        @pl.when(first)
+        def _():
+            rs_copy(0, a, 0).start()
+
+    back_rest(0)
     loads[4].wait()
     inner_rows(1)
     weight_rows(1, 1)
     sib_copy(1).start()
+
+    @pl.when(first)
+    def _():
+        rs_step(0, 1, 0)
+
     outer_rows(1)
+
+    @pl.when(first)
+    def _():
+        turn_kernel(1)
+        back_edges(1)
+
     for a in (0, 2):
         weight_rows(1, a)
         sib_copy(a).start()
-    for a in order:
+
+    sib_copy(1).wait_recv()
+
+    @pl.when(first)
+    def _():
+        rs_step(0, 0, 0)
+        rs_step(0, 2, 0)
+
+    @pl.when(second)
+    def _():
+        add_sibling(1)
+        rs_copy(0, 1, 0).start()
+        kern_copy(0).wait_recv()
+        kern_copy(1).start()
+        turn_kernel(1)
+        back_edges(1)
+
+    for a in (0, 2):
         sib_copy(a).wait_recv()
 
         @pl.when(second)
@@ -278,47 +331,66 @@
             add_sibling(a)
             rs_copy(0, a, 0).start()
 
-    @pl.when(first)
-    def _():
-        for a in order:
-            rs_step(0, a, 0)
-
-    kern_copy(0).wait_recv()
-    kern_copy(1).start()
-    turn_kernel(1)
-    back(1)
+    back_rest(1)
     loads[5].wait()
     loads[6].wait()
     inner_rows(2)
     weight_rows(2, 1)
     rs_copy(1, 1, 0).start()
 
+    @pl.when(first)
+    def _():
+        for k in range(1, bits - 1):
+            rs_step(0, 1, k)
+
     @pl.when(second)
     def _():
-        for a in order:
-            rs_step(0, a, 0)
-
-    for k in range(1, bits - 1):
-        for a in order:
-            rs_step(0, a, k)
+        rs_step(0, 1, 0)
+
     outer_rows(2)
     for a in (0, 2):
         weight_rows(2, a)
         rs_copy(1, a, 0).start()
+
+    @pl.when(first)
+    def _():
+        for k in range(1, bits - 1):
+            rs_step(0, 0, k)
+            rs_step(0, 2, k)
+        kern_copy(1).wait_recv()
+        turn_kernel(2)
+        back(2)
+        rs_step(1, 1, 0)
+
+    @pl.when(second)
+    def _():
+        for k in range(1, bits - 1):
+            rs_step(0, 1, k)
+        rs_step(0, 0, 0)
+        rs_step(0, 2, 0)
+        rs_step(1, 1, 0)
+        for k in range(1, bits - 1):
+            rs_step(0, 0, k)
+            rs_step(0, 2, k)
+
+    for a in (0, 2):
+        rs_step(1, a, 0)
+    for k in range(1, bits - 1):
+        rs_step(1, 1, k)
     for a in order:
         rs_last(0, a)
     held_copy.start()
-    rs_step(1, 1, 0)
-    kern_copy(1).wait_recv()
-    turn_kernel(2)
-    back(2)
-    rs_step(1, 0, 0)
+
+    @pl.when(second)
+    def _():
+        kern_copy(1).wait_recv()
+        turn_kernel(2)
+        back(2)
+
     for k in range(1, bits - 1):
-        rs_step(1, 1, k)
-    rs_step(1, 2, 0)
-    for k in range(1, bits - 1):
-        rs_step(1, 0, k)
-        rs_step(1, 2, k)
+        for a in (0, 2):
+            rs_step(1, a, k)
+
     held_copy.wait_recv()
     for a in order:
         rs_last(1, a)

time: 60.6 us -> 56.8 us (0.937)
  Pallas kernels: 56.3 us -> 52.7 us
    pallas_call x1, Pallas kernels: 56.3 us -> 52.7 us  [shards(): pl.pallas_call(functools.partial(kernel, (peers, cycle, height, ch, cols,...]
where the time goes in v1:
time: 56.8 us; the launch traced here: 56.7 us
  Pallas kernels  52.7 us (93%)
  local copies, waits for them, and re-layouts  3.35 us (6%)
  between operations  0.65 us (1%)
    pallas_call x1, Pallas kernels, shards(): pl.pallas_call(functools.partial(kernel, (peers, cycle, height, ch, cols,...  52.7 us
    unnamed x4, local copies, waits for them, and re-layouts  3.35 us

profile of v1, /device:TPU:1, one launch (start us, length us, event | category | flops | bytes accessed | tf_op | source)
XLA Modules:
  0.0 56.7 jit_solution(8133107560593870146)
XLA Ops:
  0.6 52.7 %shard_map.68 = (bf16[3,1,4,256,256]{4,3,2,1,0:T(8,128)(2,1)}, bf16[1,9,32,256]{3,2,1,0:T(8,128)(2,1)}) custom-call(bf16[1,9,256,256]{3,2,1,0:T(8,128)(2,1)} %bitcast.3, bf16[1,9,32,256]{3,2,1,0:T(8,128)(2,1)} %bitcast.4, bf16[3,1,4,256,256]{4,3,2,1,0:T(8,128)(2,1)} %saved_hbm.1, bf16[1,4,256,256]{3,2,1,0:T(8,128)(2,1)} %cot_hbm.1, ...), custom_call_target="tpu_custom_call" | custom-call | tf_op jit(solution)/shard_map/pallas_call | solution.py:429
  53.3 0.0 copy-start
  53.3 2.7 %copy.9 = bf16[3,1,4,256,256]{4,3,2,1,0:T(8,128)(2,1)} copy(bf16[3,1,4,256,256]{4,3,2,1,0:T(8,128)(2,1)} %get-tuple-element.8) | data formatting | bytes 3145728
  56.0 0.0 copy-done
  56.0 0.7 %copy.10 = bf16[1,32,9,256]{3,1,2,0:T(8,128)(2,1)} copy(bf16[1,32,9,256]{3,1,2,0:T(8,128)(2,1)S(1)} %bitcast.5) | data formatting | bytes 294912
Async XLA Ops:
  53.3 2.7 %copy-start = (bf16[1,9,32,256]{3,2,1,0:T(8,128)(2,1)S(1)}, bf16[1,9,32,256]{3,2,1,0:T(8,128)(2,1)}, u32[]{:S(2)}) copy-start(bf16[1,9,32,256]{3,2,1,0:T(8,128)(2,1)} %get-tuple-element.5) | copy-start | bytes 442372

commit v2 on v1

--- a/solution.py
+++ b/solution.py
@@ -13,7 +13,9 @@
 BF16 = jnp.bfloat16
 
 
-LATE = {(0, 0): (0, 1, 2), (0, 1): (0, 1, 2), (1, 0): (), (1, 1): ()}
+LATE = {(0, 0): (0, 1, 2), (0, 1): (0, 1, 2), (1, 0): (2,), (1, 1): (2,)}
+EARLY = (1, 0)
+TURN = (2, 0)
 
 
 def halving(bits, t, core, a):
@@ -25,9 +27,9 @@
 
 
 def kernel(
-    shape, w_hbm, acc_hbm, saved_hbm, cot_hbm, fresh_hbm, states_hbm, out_ref,
-    kern, kern_t, sv, cur, fresh, xs, gs, halo, states, dk, rx, part, sib, held, held_rx,
-    load_sem, halo_send, halo_recv, k_send, k_recv, rs_send, rs_recv, acc_send, acc_recv, sib_send, sib_recv, st_sem,
+    shape, w_hbm, acc_hbm, saved_hbm, cot_hbm, fresh_hbm, states, out_ref,
+    kern, kern_t, sv, cur, fresh, xs, gs, halo, dk, rx, part, sib, held, held_rx, early,
+    load_sem, halo_send, halo_recv, k_send, k_recv, rs_send, rs_recv, acc_send, acc_recv, sib_send, sib_recv, early_send, early_recv,
 ):
     peers, cycle, height, ch, cols, scale = shape
     bits = peers.bit_length() - 1
@@ -119,6 +121,16 @@
             device_id_type=MESH,
         )
 
+    def early_copy(a):
+        return pltpu.make_async_remote_copy(
+            src_ref=dk.at[0, a],
+            dst_ref=early.at[a],
+            send_sem=early_send.at[a],
+            recv_sem=early_recv.at[a],
+            device_id={"blk": far},
+            device_id_type=MESH,
+        )
+
     wide = 3 * ch
     lane = lax.broadcasted_iota(jnp.int32, (ch, cols), 1)
 
@@ -161,7 +173,7 @@
         base = pl.multiple_of(r * wide, wide)
         total = jnp.dot(kern_t[...], gs[pl.ds(base, 3 * wide), :], preferred_element_type=F32)
         value = jnp.where(sv[t, r].astype(F32) > 0, total, 0.0).astype(BF16)
-        states[t, r] = value
+        states[t, 0, r] = value
         if t + 1 < TICKS:
             cur[t + 1, r] = jnp.where(restart[t + 1], fresh[t, r], value)
 
@@ -180,7 +192,6 @@
             return carry
 
         lax.fori_loop(0, height - 2, inner, 0)
-        pltpu.make_async_copy(states.at[t], states_hbm.at[t, 0], st_sem.at[t]).start()
 
     def back(t):
         back_edges(t)
@@ -188,7 +199,10 @@
 
     slab = ch // peers
 
-    slot = (((0, 0), (0, 1)), ((0, 1), (1, 0)), ((1, 0), (1, 1)))
+    odd_slot = ((0, 1), (1, 0), (1, 1))
+
+    def even_slot(t, a):
+        return ((1, 0) if a in EARLY else (0, 0), (0, 1), (1, 0))[t]
 
     def pick(even, odd):
         return even if even == odd else even + core * (odd - even)
@@ -207,9 +221,11 @@
             for j in range(peers):
                 at = b * ch + j * slab
                 value = total[at : at + slab, :]
-                at = pick(place(bits, *slot[t][0], a, j), place(bits, *slot[t][1], a, j))
+                at = pick(place(bits, *even_slot(t, a), a, j), place(bits, *odd_slot[t], a, j))
                 if t == TICKS - 1:
                     extra = sib[a, at, b].astype(F32)
+                    if a in EARLY:
+                        extra = extra + early[a, at, b].astype(F32)
                     value = value + jnp.where(core == 0, extra, 0.0)
                 dk[t, a, at, b] = value.astype(BF16)
 
@@ -261,6 +277,16 @@
     first = core == 0
     second = core == 1
 
+    def launch(a):
+        @pl.when(first)
+        def _():
+            if a in EARLY:
+                early_copy(a).start()
+            else:
+                rs_copy(0, a, 0).start()
+
+    rest = [a for a in order if a not in EARLY]
+
     loads[0].wait()
     halo_start(0)
     loads[2].wait()
@@ -269,33 +295,24 @@
     loads[1].wait()
     inner_rows(0)
     weight_rows(0, 1)
+    launch(1)
     loads[3].wait()
-
-    @pl.when(first)
-    def _():
-        rs_copy(0, 1, 0).start()
-        kern_copy(0).wait_recv()
-        kern_copy(1).start()
-
     outer_rows(0)
     back_edges(0)
     for a in (0, 2):
         weight_rows(0, a)
-
-        @pl.when(first)
-        def _():
-            rs_copy(0, a, 0).start()
+        launch(a)
+
+    @pl.when(first)
+    def _():
+        kern_copy(0).wait_recv()
+        kern_copy(1).start()
 
     back_rest(0)
     loads[4].wait()
     inner_rows(1)
     weight_rows(1, 1)
     sib_copy(1).start()
-
-    @pl.when(first)
-    def _():
-        rs_step(0, 1, 0)
-
     outer_rows(1)
 
     @pl.when(first)
@@ -311,8 +328,8 @@
 
     @pl.when(first)
     def _():
-        rs_step(0, 0, 0)
-        rs_step(0, 2, 0)
+        for a in rest:
+            rs_step(0, a, 0)
 
     @pl.when(second)
     def _():
@@ -335,30 +352,39 @@
     loads[5].wait()
     loads[6].wait()
     inner_rows(2)
-    weight_rows(2, 1)
-    rs_copy(1, 1, 0).start()
-
-    @pl.when(first)
-    def _():
-        for k in range(1, bits - 1):
-            rs_step(0, 1, k)
-
-    @pl.when(second)
-    def _():
-        rs_step(0, 1, 0)
-
-    outer_rows(2)
-    for a in (0, 2):
+
+    def last_rows(a):
+        if a in EARLY:
+            @pl.when(first)
+            def _():
+                early_copy(a).wait_recv()
+
         weight_rows(2, a)
         rs_copy(1, a, 0).start()
 
+    last_rows(1)
+
     @pl.when(first)
     def _():
         for k in range(1, bits - 1):
-            rs_step(0, 0, k)
-            rs_step(0, 2, k)
+            for a in rest:
+                rs_step(0, a, k)
+
+    @pl.when(second)
+    def _():
+        rs_step(0, 1, 0)
+
+    outer_rows(2)
+    @pl.when(first)
+    def _():
         kern_copy(1).wait_recv()
         turn_kernel(2)
+
+    for a in (0, 2):
+        last_rows(a)
+
+    @pl.when(first)
+    def _():
         back(2)
         rs_step(1, 1, 0)
 
@@ -373,13 +399,28 @@
             rs_step(0, 0, k)
             rs_step(0, 2, k)
 
-    for a in (0, 2):
+    for a in TURN:
         rs_step(1, a, 0)
     for k in range(1, bits - 1):
         rs_step(1, 1, k)
-    for a in order:
-        rs_last(0, a)
+
+    @pl.when(first)
+    def _():
+        for a in EARLY:
+            held[1, 3 * a : 3 * a + 3] = held[0, 3 * a : 3 * a + 3]
+        for a in rest:
+            rs_last(0, a)
+
+    @pl.when(second)
+    def _():
+        for a in order:
+            rs_last(0, a)
+
     held_copy.start()
+
+    for k in range(1, bits - 1):
+        for a in TURN:
+            rs_step(1, a, k)
 
     @pl.when(second)
     def _():
@@ -387,16 +428,11 @@
         turn_kernel(2)
         back(2)
 
-    for k in range(1, bits - 1):
-        for a in (0, 2):
-            rs_step(1, a, k)
-
     held_copy.wait_recv()
-    for a in order:
+    for a in (1, *TURN):
         rs_last(1, a)
 
     for t in range(TICKS):
-        pltpu.make_async_copy(states.at[t], states_hbm.at[t, 0], st_sem.at[t]).wait()
         @pl.when(has_up)
         def _():
             halo_copy(t, 1).wait_send()
@@ -407,12 +443,26 @@
 
     for t in range(TICKS - 1):
         kern_copy(t).wait_send()
+    for a in range(3):
+        sib_copy(a).wait_send()
+        for k in range(bits):
+            rs_copy(1, a, k).wait_send()
+    held_copy.wait_send()
+
+    @pl.when(first)
+    def _():
+        for a in range(3):
+            if a in EARLY:
+                early_copy(a).wait_send()
+            else:
+                for k in range(bits):
+                    rs_copy(0, a, k).wait_send()
+
+    @pl.when(second)
+    def _():
         for a in range(3):
             for k in range(bits):
-                rs_copy(t, a, k).wait_send()
-    for a in range(3):
-        sib_copy(a).wait_send()
-    held_copy.wait_send()
+                rs_copy(0, a, k).wait_send()
 
 
 def shards(section_weights, grad_acc, saved_inputs, cotangent, fresh_grads):
@@ -429,11 +479,11 @@
     states, out = pl.pallas_call(
         functools.partial(kernel, (peers, cycle, height, ch, cols, scale)),
         out_shape=(
-            jax.ShapeDtypeStruct(saved_inputs.shape, BF16),
-            jax.ShapeDtypeStruct(held.shape, BF16),
+            pltpu.VMEM(saved_inputs.shape, BF16),
+            pltpu.VMEM(held.shape, BF16),
         ),
         in_specs=[anywhere] * 5,
-        out_specs=(anywhere, pl.BlockSpec(memory_space=pltpu.VMEM)),
+        out_specs=(pl.BlockSpec(memory_space=pltpu.VMEM), pl.BlockSpec(memory_space=pltpu.VMEM)),
         scratch_shapes=[
             pltpu.VMEM((ticks, 9, ch, ch), BF16),
             pltpu.VMEM((ch, 9 * ch), BF16),
@@ -443,13 +493,13 @@
             pltpu.VMEM((ch, height * cols), BF16),
             pltpu.VMEM(((height + 2) * 3 * ch, cols), BF16),
             pltpu.VMEM((ticks, 2, ch, cols), BF16),
-            pltpu.VMEM((ticks, height, ch, cols), BF16),
             pltpu.VMEM((ticks, 3, peers, 3, slab, ch), BF16),
             pltpu.VMEM((2, 3, peers, 3, slab, ch), BF16),
             pltpu.VMEM((2, 3, peers, 3, slab, ch), BF16),
             pltpu.VMEM((3, peers, 3, slab, ch), BF16),
             pltpu.VMEM((2, 9, slab, ch), BF16),
             pltpu.VMEM((9, slab, ch), BF16),
+            pltpu.VMEM((3, peers, 3, slab, ch), BF16),
             dma((7,)),
             dma((ticks, 2)),
             dma((ticks, 2)),
@@ -461,7 +511,8 @@
             dma,
             dma((3,)),
             dma((3,)),
-            dma((ticks,)),
+            dma((3,)),
+            dma((3,)),
         ],
         compiler_params=pltpu.CompilerParams(collective_id=0, has_side_effects=True),
     )(weights, held, saved_inputs, cotangent, fresh_grads)

time: 56.8 us -> 53.3 us (0.938)
  Pallas kernels: 52.7 us -> 50.7 us
  local copies, waits for them, and re-layouts: 3.35 us -> 1.81 us
    pallas_call x1, Pallas kernels: 52.7 us -> 50.7 us  [shards(): pl.pallas_call(functools.partial(kernel, (peers, cycle, height, ch, cols,...]
    unnamed x4 -> x2, local copies, waits for them, and re-layouts: 3.35 us -> 1.81 us
where the time goes in v2:
time: 53.3 us; the launch traced here: 53.2 us
  Pallas kernels  50.7 us (95%)
  local copies, waits for them, and re-layouts  1.81 us (3%)
  between operations  0.64 us (1%)
    pallas_call x1, Pallas kernels, shards(): pl.pallas_call(functools.partial(kernel, (peers, cycle, height, ch, cols,...  50.7 us
    unnamed x2, local copies, waits for them, and re-layouts  1.81 us

profile of v2, /device:TPU:1, one launch (start us, length us, event | category | flops | bytes accessed | tf_op | source)
XLA Modules:
  0.0 53.2 jit_solution(6576249057348203263)
XLA Ops:
  0.6 50.7 %shard_map.68 = (bf16[3,1,4,256,256]{4,3,2,1,0:T(8,128)(2,1)S(1)}, bf16[1,9,32,256]{3,2,1,0:T(8,128)(2,1)S(1)}) custom-call(bf16[1,9,256,256]{3,2,1,0:T(8,128)(2,1)} %bitcast.4, bf16[1,9,32,256]{3,2,1,0:T(8,128)(2,1)} %bitcast.5, bf16[3,1,4,256,256]{4,3,2,1,0:T(8,128)(2,1)} %saved_hbm.1, bf16[1,4,256,256]{3,2,1,0:T(8,128)(2,1)} %cot_hbm.1, ...), custom_call_target="tpu_custom_call" | custom-call | tf_op jit(solution)/shard_map/pallas_call | solution.py:479
  51.4 1.1 %copy.9 = bf16[3,1,4,256,256]{4,3,2,1,0:T(8,128)(2,1)} copy(bf16[3,1,4,256,256]{4,3,2,1,0:T(8,128)(2,1)S(1)} %get-tuple-element.6) | data formatting | bytes 3145728
  52.5 0.7 %copy.10 = bf16[1,32,9,256]{3,1,2,0:T(8,128)(2,1)} copy(bf16[1,32,9,256]{3,1,2,0:T(8,128)(2,1)S(1)} %bitcast.3) | data formatting | bytes 294912

commit v3 on v2

--- a/solution.py
+++ b/solution.py
@@ -463,6 +463,16 @@
         for a in range(3):
             for k in range(bits):
                 rs_copy(0, a, k).wait_send()
+
+
+def store(states, out, states_hbm, out_hbm, sem):
+    copies = [pltpu.make_async_copy(out, out_hbm, sem.at[0])]
+    for t in range(TICKS):
+        copies.append(pltpu.make_async_copy(states.at[t], states_hbm.at[t], sem.at[t + 1]))
+    for copy in copies:
+        copy.start()
+    for copy in copies:
+        copy.wait()
 
 
 def shards(section_weights, grad_acc, saved_inputs, cotangent, fresh_grads):
@@ -516,6 +526,19 @@
         ],
         compiler_params=pltpu.CompilerParams(collective_id=0, has_side_effects=True),
     )(weights, held, saved_inputs, cotangent, fresh_grads)
+    states = pltpu.with_memory_space_constraint(states, pltpu.VMEM)
+    out = pltpu.with_memory_space_constraint(out, pltpu.VMEM)
+    vmem = pl.BlockSpec(memory_space=pltpu.VMEM)
+    states, out = pl.pallas_call(
+        store,
+        out_shape=(
+            jax.ShapeDtypeStruct(saved_inputs.shape, BF16),
+            jax.ShapeDtypeStruct(held.shape, BF16),
+        ),
+        in_specs=[vmem, vmem],
+        out_specs=(anywhere, anywhere),
+        scratch_shapes=[dma((ticks + 1,))],
+    )(states, out)
     return states, out.transpose(0, 2, 1, 3)
 
 

time: 53.3 us -> 52.8 us (level)
  local copies, waits for them, and re-layouts: 1.81 us -> 0 us
  Pallas kernels: 50.7 us -> 52 us
    unnamed x2 -> x0, local copies, waits for them, and re-layouts: 1.81 us -> none
    pallas_call x0 -> x1, Pallas kernels: none -> 1.22 us  [shards(): pl.pallas_call(store, out_shape=(jax.ShapeDtypeStruct(saved_inputs.shape,...]
where the time goes in v3:
time: 52.8 us; the launch traced here: 52.6 us
  Pallas kernels  52 us (98%)
  between operations  0.64 us (1%)
    pallas_call x1, Pallas kernels, shards(): pl.pallas_call(functools.partial(kernel, (peers, cycle, height, ch, cols,...  50.7 us
    pallas_call x1, Pallas kernels, shards(): pl.pallas_call(store, out_shape=(jax.ShapeDtypeStruct(saved_inputs.shape,...  1.22 us

profile of v3, /device:TPU:1, one launch (start us, length us, event | category | flops | bytes accessed | tf_op | source)
XLA Modules:
  0.0 52.6 jit_solution(2461582736211362452)
XLA Ops:
  0.6 50.7 %shard_map.68 = (bf16[3,1,4,256,256]{4,3,2,1,0:T(8,128)(2,1)S(1)}, bf16[1,9,32,256]{3,2,1,0:T(8,128)(2,1)S(1)}) custom-call(bf16[1,9,256,256]{3,2,1,0:T(8,128)(2,1)} %bitcast.3, bf16[1,9,32,256]{3,2,1,0:T(8,128)(2,1)} %bitcast.4, bf16[3,1,4,256,256]{4,3,2,1,0:T(8,128)(2,1)} %saved_hbm.1, bf16[1,4,256,256]{3,2,1,0:T(8,128)(2,1)} %cot_hbm.1, ...), custom_call_target="tpu_custom_call" | custom-call | tf_op jit(solution)/shard_map/pallas_call | solution.py:489
  51.4 1.2 %shard_map.69 = (bf16[3,1,4,256,256]{4,3,2,1,0:T(8,128)(2,1)}, bf16[1,9,32,256]{3,2,1,0:T(8,128)(2,1)}) custom-call(bf16[3,1,4,256,256]{4,3,2,1,0:T(8,128)(2,1)S(1)} %get-tuple-element.6.states, bf16[1,9,32,256]{3,2,1,0:T(8,128)(2,1)S(1)} %get-tuple-element.7.out), custom_call_target="tpu_custom_call" | custom-call | tf_op jit(solution)/shard_map/pallas_call | solution.py:532

commit v4 on v3

--- a/solution.py
+++ b/solution.py
@@ -84,11 +84,15 @@
         )
 
     def halo_start(t):
+        @pl.when(jnp.logical_and(has_down, bit[0] == 1))
+        def _():
+            halo_copy(t, 0).start()
+
         @pl.when(has_up)
         def _():
             halo_copy(t, 1).start()
 
-        @pl.when(has_down)
+        @pl.when(jnp.logical_and(has_down, bit[0] == 0))
         def _():
             halo_copy(t, 0).start()
 

time: 52.8 us -> 52.8 us (level)
  no operation moved by 1% of the time
where the time goes in v4:
time: 52.8 us; the launch traced here: 52.6 us
  Pallas kernels  52 us (98%)
  between operations  0.64 us (1%)
    pallas_call x1, Pallas kernels, shards(): pl.pallas_call(functools.partial(kernel, (peers, cycle, height, ch, cols,...  50.7 us
    pallas_call x1, Pallas kernels, shards(): pl.pallas_call(store, out_shape=(jax.ShapeDtypeStruct(saved_inputs.shape,...  1.22 us

profile of v4, /device:TPU:1, one launch (start us, length us, event | category | flops | bytes accessed | tf_op | source)
XLA Modules:
  0.0 52.6 jit_solution(14545542286147417877)
XLA Ops:
  0.6 50.7 %shard_map.68 = (bf16[3,1,4,256,256]{4,3,2,1,0:T(8,128)(2,1)S(1)}, bf16[1,9,32,256]{3,2,1,0:T(8,128)(2,1)S(1)}) custom-call(bf16[1,9,256,256]{3,2,1,0:T(8,128)(2,1)} %bitcast.3, bf16[1,9,32,256]{3,2,1,0:T(8,128)(2,1)} %bitcast.4, bf16[3,1,4,256,256]{4,3,2,1,0:T(8,128)(2,1)} %saved_hbm.1, bf16[1,4,256,256]{3,2,1,0:T(8,128)(2,1)} %cot_hbm.1, ...), custom_call_target="tpu_custom_call" | custom-call | tf_op jit(solution)/shard_map/pallas_call | solution.py:493
  51.4 1.2 %shard_map.69 = (bf16[3,1,4,256,256]{4,3,2,1,0:T(8,128)(2,1)}, bf16[1,9,32,256]{3,2,1,0:T(8,128)(2,1)}) custom-call(bf16[3,1,4,256,256]{4,3,2,1,0:T(8,128)(2,1)S(1)} %get-tuple-element.6.states, bf16[1,9,32,256]{3,2,1,0:T(8,128)(2,1)S(1)} %get-tuple-element.7.out), custom_call_target="tpu_custom_call" | custom-call | tf_op jit(solution)/shard_map/pallas_call | solution.py:536
